TPU v7x, 256 devices: a whole 4x4x8 slice. The times are simulated.
256 devices in a mesh: dp: 32 (over z_hi, x, core), seq: 8 (over y, z_lo).
Axes of the slice: x: 4, y: 4, z: 8 (z_hi: 4, z_lo: 2; z = z_hi * 2 + z_lo), core: 2. Of those that a mesh axis runs over, the one named last changes fastest.
Arguments:
- q_proj: bfloat16 [32, 1024, 4096], P('dp', 'seq'), may hold values from -200 to 200
- k_proj: bfloat16 [32, 1024, 512], P('dp', 'seq'), may hold values from -6 to 6
- v_proj: bfloat16 [32, 1024, 512], P('dp', 'seq'), may hold values from -6 to 6
- cache_k: bfloat16 [32, 1024, 512], P('dp', 'seq'), may hold values from -6 to 6
- cache_v: bfloat16 [32, 1024, 512], P('dp', 'seq'), may hold values from -6 to 6
- bias_q: bfloat16 [4096], replicated, may hold values from -3 to 3
- bias_k: bfloat16 [512], replicated, may hold values from -3 to 3
- bias_v: bfloat16 [512], replicated, may hold values from -3 to 3
- start: int32 [32], P('dp'), may hold values from 256 to 1024, as said below
- dout: bfloat16 [32, 1024, 4096], P('dp', 'seq'), may hold values from -6 to 6
Outputs:
- attn_out: bfloat16 [32, 1024, 4096], P('dp', 'seq')
- grad_q: bfloat16 [32, 1024, 4096], P('dp', 'seq')
- grad_k: bfloat16 [32, 1024, 512], P('dp', 'seq')
- grad_v: bfloat16 [32, 1024, 512], P('dp', 'seq')
- grad_bias_q: float32 [4096], replicated
- grad_bias_k: float32 [512], replicated
- grad_bias_v: float32 [512], replicated
Inputs may be any that keep to these rules, and one draw needn't show every extreme that they name: Cache slots at and beyond start hold no prefix; some sequence has a full prefix of 1024 slots.
All inputs are finite; a program needn't handle non-finite values.
Results may differ from a plain program's by a relative error of at most 0.04.
The roundings to bfloat16 on the way count: a program that leaves them out, or rounds other values in their place, can miss the bound.
Values may be sent and summed in bfloat16 or wider, within the bound.
A program may use at most 128 MiB of HBM per device.

v0:
```python
import jax
import jax.numpy as jnp
from jax import lax
from jax.sharding import PartitionSpec as P

HQ = 32
KV = 4
HD = 128
GROUP = 8


def rotary_tables(positions, width):
    half = width // 2
    freqs = jnp.exp(
        -(2.0 * jnp.arange(half, dtype=jnp.float32) / width) * jnp.log(jnp.float32(1000000.0))
    )
    angles = positions.astype(jnp.float32)[:, None] * freqs[None, :]
    cosine = jnp.concatenate([jnp.cos(angles), jnp.cos(angles)], axis=1)
    sine = jnp.concatenate([jnp.sin(angles), jnp.sin(angles)], axis=1)
    return (cosine[:, None, :], sine[:, None, :])


def rotary(values, positions):
    cosine, sine = rotary_tables(positions, values.shape[2])
    half = values.shape[2] // 2
    turned = jnp.concatenate([-values[:, :, half:], values[:, :, :half]], axis=2)
    return values * cosine + turned * sine


def rotary_back(grads, positions):
    cosine, sine = rotary_tables(positions, grads.shape[2])
    half = grads.shape[2] // 2
    scaled = grads * sine
    turned = jnp.concatenate([scaled[:, :, half:], -scaled[:, :, :half]], axis=2)
    return grads * cosine + turned


def attend(queries, cotangent, keys, values, first, row_zero, prefix):
    rows, heads, width = queries.shape
    key_count = keys.shape[0]
    slab = key_count - prefix
    head_block = max(1, min(512 // rows, GROUP, heads))
    row_block = min(rows, 512)
    scale = width ** (-0.5)
    key_index = jnp.arange(key_count, dtype=jnp.int32)

    def head_step(carry, head_slot):
        key_acc, value_acc = carry
        head_zero = head_slot * head_block
        owner = head_zero // GROUP
        key_one = lax.dynamic_index_in_dim(keys, owner, 1, keepdims=False)
        value_one = lax.dynamic_index_in_dim(values, owner, 1, keepdims=False)
        query_part = lax.dynamic_slice_in_dim(queries, head_zero, head_block, 1)
        cot_part = lax.dynamic_slice_in_dim(cotangent, head_zero, head_block, 1)

        def row_step(inner, row_slot):
            grad_key, grad_value = inner
            offset = row_slot * row_block
            query_rows = lax.dynamic_slice_in_dim(query_part, offset, row_block, 0)
            cot_rows = lax.dynamic_slice_in_dim(cot_part, offset, row_block, 0)
            query_index = row_zero + offset + jnp.arange(row_block, dtype=jnp.int32)
            allowed = jnp.where(
                key_index[None, :] < prefix,
                key_index[None, :] < first,
                key_index[None, :] - prefix <= query_index[:, None],
            )
            scores = (
                jnp.einsum("rhd,kd->hrk", query_rows, key_one, preferred_element_type=jnp.float32)
                * scale
            )
            scores = jnp.where(allowed[None], scores, -1e30)
            highest = jnp.max(scores, axis=-1, keepdims=True)
            expo = jnp.exp(scores - highest)
            probs = expo / jnp.sum(expo, axis=-1, keepdims=True)
            probs_b = probs.astype(jnp.bfloat16)
            output = jnp.einsum(
                "hrk,kd->rhd", probs_b, value_one, preferred_element_type=jnp.float32
            ).astype(jnp.bfloat16)
            delta = jnp.sum(cot_rows.astype(jnp.float32) * output.astype(jnp.float32), axis=-1).T
            dprobs = jnp.einsum(
                "rhd,kd->hrk", cot_rows, value_one, preferred_element_type=jnp.float32
            )
            dscore = (probs * (dprobs - delta[:, :, None])).astype(jnp.bfloat16)
            grad_query = (
                jnp.einsum("hrk,kd->rhd", dscore, key_one, preferred_element_type=jnp.float32)
                * scale
            ).astype(jnp.bfloat16)
            grad_key = (
                grad_key
                + jnp.einsum(
                    "hrk,rhd->kd",
                    dscore[:, :, prefix:],
                    query_rows,
                    preferred_element_type=jnp.float32,
                )
                * scale
            )
            grad_value = grad_value + jnp.einsum(
                "hrk,rhd->kd", probs_b[:, :, prefix:], cot_rows, preferred_element_type=jnp.float32
            )
            return ((grad_key, grad_value), (output, grad_query))

        empty = jnp.zeros((slab, width), jnp.float32)
        (grad_key, grad_value), (outputs, grads) = lax.scan(
            row_step, (empty, empty), jnp.arange(rows // row_block, dtype=jnp.int32)
        )
        outputs = outputs.reshape(rows, head_block, width)
        grads = grads.reshape(rows, head_block, width)
        old_key = lax.dynamic_index_in_dim(key_acc, owner, 1, keepdims=False)
        old_value = lax.dynamic_index_in_dim(value_acc, owner, 1, keepdims=False)
        key_acc = lax.dynamic_update_index_in_dim(key_acc, old_key + grad_key, owner, 1)
        value_acc = lax.dynamic_update_index_in_dim(value_acc, old_value + grad_value, owner, 1)
        return ((key_acc, value_acc), (outputs, grads))

    zeros_kv = jnp.zeros((slab, keys.shape[1], width), jnp.float32)
    (key_acc, value_acc), (outputs, grads) = lax.scan(
        head_step, (zeros_kv, zeros_kv), jnp.arange(heads // head_block, dtype=jnp.int32)
    )
    outputs = jnp.transpose(outputs, (1, 0, 2, 3)).reshape(rows, heads, width)
    grads = jnp.transpose(grads, (1, 0, 2, 3)).reshape(rows, heads, width)
    return (outputs, grads, key_acc, value_acc)


def body(q_proj, k_proj, v_proj, cache_k, cache_v, bias_q, bias_k, bias_v, start, dout):
    devices = lax.axis_size("seq")
    rank = lax.axis_index("seq")
    tokens = q_proj.shape[1]
    first = start[0]
    positions = first + rank * tokens + jnp.arange(tokens, dtype=jnp.int32)
    queries = rotary(
        (q_proj[0].astype(jnp.float32) + bias_q.astype(jnp.float32)).reshape(tokens, HQ, HD),
        positions,
    ).astype(jnp.bfloat16)
    keys = rotary(
        (k_proj[0].astype(jnp.float32) + bias_k.astype(jnp.float32)).reshape(tokens, KV, HD),
        positions,
    ).astype(jnp.bfloat16)
    values = (
        (v_proj[0].astype(jnp.float32) + bias_v.astype(jnp.float32))
        .astype(jnp.bfloat16)
        .reshape(tokens, KV, HD)
    )
    cotangent = dout[0].reshape(tokens, HQ, HD)
    cached_keys = cache_k[0].reshape(cache_k.shape[1], KV, HD)
    cached_values = cache_v[0].reshape(cache_v.shape[1], KV, HD)
    copies = max(devices // KV, 1)
    keys_wide = jnp.repeat(keys, copies, axis=1)
    values_wide = jnp.repeat(values, copies, axis=1)
    cache_keys_wide = jnp.repeat(cached_keys, copies, axis=1)
    cache_values_wide = jnp.repeat(cached_values, copies, axis=1)
    head_queries, head_keys, head_values, head_cot = (
        lax.all_to_all(queries, "seq", split_axis=1, concat_axis=0, tiled=True),
        lax.all_to_all(keys_wide, "seq", split_axis=1, concat_axis=0, tiled=True),
        lax.all_to_all(values_wide, "seq", split_axis=1, concat_axis=0, tiled=True),
        lax.all_to_all(cotangent, "seq", split_axis=1, concat_axis=0, tiled=True),
    )
    head_cache_keys, head_cache_values = (
        lax.all_to_all(cache_keys_wide, "seq", split_axis=1, concat_axis=0, tiled=True),
        lax.all_to_all(cache_values_wide, "seq", split_axis=1, concat_axis=0, tiled=True),
    )
    prefix = head_cache_keys.shape[0]
    all_keys = jnp.concatenate([head_cache_keys, head_keys], axis=0)
    all_values = jnp.concatenate([head_cache_values, head_values], axis=0)
    outputs, dq_rot, dk_rot, dv_all = attend(
        head_queries, head_cot, all_keys, all_values, first, 0, prefix
    )
    out_tokens, dq_tokens = (
        lax.all_to_all(outputs, "seq", split_axis=0, concat_axis=1, tiled=True),
        lax.all_to_all(dq_rot, "seq", split_axis=0, concat_axis=1, tiled=True),
    )
    dk_copies, dv_copies = (
        lax.all_to_all(
            dk_rot.astype(jnp.bfloat16), "seq", split_axis=0, concat_axis=1, tiled=True
        ).astype(dk_rot.dtype),
        lax.all_to_all(
            dv_all.astype(jnp.bfloat16), "seq", split_axis=0, concat_axis=1, tiled=True
        ).astype(dv_all.dtype),
    )
    dk_tokens = jnp.sum(dk_copies.reshape(tokens, KV, copies, HD), axis=2)
    dv_tokens = jnp.sum(dv_copies.reshape(tokens, KV, copies, HD), axis=2)
    grad_query = rotary_back(dq_tokens.astype(jnp.float32), positions)
    grad_key = rotary_back(dk_tokens, positions)
    sums_query, sums_key, sums_value = lax.psum(
        (
            jnp.sum(grad_query, axis=0).reshape(HQ * HD),
            jnp.sum(grad_key, axis=0).reshape(KV * HD),
            jnp.sum(dv_tokens, axis=0).reshape(KV * HD),
        ),
        ("dp", "seq"),
    )
    return (
        out_tokens.reshape(1, tokens, HQ * HD),
        grad_query.astype(jnp.bfloat16).reshape(1, tokens, HQ * HD),
        grad_key.astype(jnp.bfloat16).reshape(1, tokens, KV * HD),
        dv_tokens.astype(jnp.bfloat16).reshape(1, tokens, KV * HD),
        sums_query,
        sums_key,
        sums_value,
    )


def solution(mesh):
    placed = (
        P("dp", "seq", None),
        P("dp", "seq", None),
        P("dp", "seq", None),
        P("dp", "seq", None),
        P("dp", "seq", None),
        P(),
        P(),
        P(),
        P("dp"),
        P("dp", "seq", None),
    )
    return jax.shard_map(
        body,
        mesh=mesh,
        in_specs=placed,
        out_specs=(
            P("dp", "seq", None),
            P("dp", "seq", None),
            P("dp", "seq", None),
            P("dp", "seq", None),
            P(),
            P(),
            P(),
        ),
        check_vma=False,
    )
```

profile of v0, /device:TPU:1, one launch (start us, length us, event | category | flops | bytes accessed | tf_op | source)
XLA Modules:
  0.0 376.5 jit_solution(17324488417311112449)
XLA Ops:
  2.4 6.5 %all-to-all-start.2 = ((bf16[128,8,128]{2,0,1:T(8,128)(2,1)}), bf16[128,8,128]{2,0,1:T(8,128)(2,1)S(1)}, u32[]{:S(2)}, u32[]{:S(2)}) async-start(bf16[128,8,128]{2,0,1:T(8,128)(2,1)} %bitcast.11), calls=%async_computation.2 | async-start | bytes 524288 | tf_op jit(solution)/shard_map/all_to_all | solution.py:158
  12.1 3.0 all-to-all-done.2
  15.8 3.4 all-to-all-start.4
  19.3 6.0 %all-to-all-done.4 = bf16[128,8,128]{2,0,1:T(8,128)(2,1)S(1)} async-done(((bf16[128,8,128]{2,0,1:T(8,128)(2,1)}), bf16[128,8,128]{2,0,1:T(8,128)(2,1)S(1)}, u32[]{:S(2)}, u32[]{:S(2)}) %all-to-all-start.4) | async-done | bytes 262176 | tf_op jit(solution)/shard_map/all_to_all | solution.py:159
  26.1 3.4 all-to-all-start.5
  29.8 5.8 %all-to-all-done.5 = bf16[128,8,128]{2,0,1:T(8,128)(2,1)S(1)} async-done(((bf16[128,8,128]{2,0,1:T(8,128)(2,1)}), bf16[128,8,128]{2,0,1:T(8,128)(2,1)S(1)}, u32[]{:S(2)}, u32[]{:S(2)}) %all-to-all-start.5) | async-done | bytes 262176 | tf_op jit(solution)/shard_map/all_to_all | solution.py:154
  36.4 3.4 all-to-all-start.3
  41.2 4.7 %all-to-all-done.3 = bf16[128,8,128]{2,0,1:T(8,128)(2,1)S(1)} async-done(((bf16[128,8,128]{2,0,1:T(8,128)(2,1)}), bf16[128,8,128]{2,0,1:T(8,128)(2,1)S(1)}, u32[]{:S(2)}, u32[]{:S(2)}) %all-to-all-start.3) | async-done | bytes 262176 | tf_op jit(solution)/shard_map/all_to_all | solution.py:153
  45.9 3.7 all-to-all-start.1
  52.2 1.3 copy.142
  53.5 6.5 %all-to-all-done.1 = bf16[128,32,128]{0,2,1:T(8,128)(2,1)S(1)} async-done(((bf16[128,32,128]{0,2,1:T(8,128)(2,1)}), bf16[128,32,128]{0,2,1:T(8,128)(2,1)S(1)}, u32[]{:S(2)}, u32[]{:S(2)}) %all-to-all-start.1) | async-done | bytes 1048608 | tf_op jit(solution)/shard_map/all_to_all | solution.py:155
  60.0 3.6 all-to-all-start
  63.6 1.8 pad_maximum_fusion.1
  66.7 7.2 %all-to-all-done = bf16[128,32,128]{2,0,1:T(8,128)(2,1)S(1)} async-done(((bf16[128,32,128]{2,0,1:T(8,128)(2,1)}), bf16[128,32,128]{2,0,1:T(8,128)(2,1)S(1)}, u32[]{:S(2)}, u32[]{:S(2)}) %all-to-all-start) | async-done | bytes 1048608 | tf_op jit(solution)/shard_map/all_to_all | solution.py:152
  75.0 139.6 %while.59 = (s32[]{:T(128)}, f32[1024,1,128]{2,0,1:T(8,128)S(1)}, f32[1024,1,128]{2,0,1:T(8,128)S(1)}, bf16[4,1024,1,128]{3,1,2,0:T(8,128)(2,1)}, bf16[4,1024,1,...) while((s32[]{:T(128)}, f32[1024,1,128]{2,0,1:T(8,128)S(1)}, ...), condition=%wide.region_6.7_spmd.clone.clone, body=%wide.region_0.6_spmd.clone.clone.sunk | while | flops 1359287296 | bytes 49224388 | solution.py:116
  79.6 28.5 %while.60 = (s32[]{:T(128)}, f32[1024,128]{1,0:T(8,128)S(1)}, f32[1024,128]{1,0:T(8,128)S(1)}, bf16[2,512,1,128]{3,1,0,2:T(8,128)(2,1)}, bf16[2,512,1,128]{3,1,2...) while((s32[]{:T(128)}, f32[1024,128]{1,0:T(8,128)S(1)}, ...), condition=%wide.region_5.5_spmd.clone.clone, body=%wide.region_1.4_spmd.clone.clone.sunk | while | flops 1359025152 | bytes 41875732 | solution.py:104
  81.6 2.3 fusion.76
  86.9 2.4 fusion.79
  90.1 3.1 fusion.81
  95.9 2.3 fusion.76
  101.1 2.4 fusion.79
  104.4 3.1 fusion.81
  114.5 28.5 %while.60 = (s32[]{:T(128)}, f32[1024,128]{1,0:T(8,128)S(1)}, f32[1024,128]{1,0:T(8,128)S(1)}, bf16[2,512,1,128]{3,1,0,2:T(8,128)(2,1)}, bf16[2,512,1,128]{3,1,2...) while((s32[]{:T(128)}, f32[1024,128]{1,0:T(8,128)S(1)}, ...), condition=%wide.region_5.5_spmd.clone.clone, body=%wide.region_1.4_spmd.clone.clone.sunk | while | flops 1359025152 | bytes 41875732 | solution.py:104
  116.5 2.3 fusion.76
  121.8 2.4 fusion.79
  125.0 3.1 fusion.81
  130.8 2.3 fusion.76
  136.0 2.4 fusion.79
  139.3 3.1 fusion.81
  149.4 28.5 %while.60 = (s32[]{:T(128)}, f32[1024,128]{1,0:T(8,128)S(1)}, f32[1024,128]{1,0:T(8,128)S(1)}, bf16[2,512,1,128]{3,1,0,2:T(8,128)(2,1)}, bf16[2,512,1,128]{3,1,2...) while((s32[]{:T(128)}, f32[1024,128]{1,0:T(8,128)S(1)}, ...), condition=%wide.region_5.5_spmd.clone.clone, body=%wide.region_1.4_spmd.clone.clone.sunk | while | flops 1359025152 | bytes 41875732 | solution.py:104
  151.5 2.3 fusion.76
  156.7 2.4 fusion.79
  159.9 3.1 fusion.81
  165.7 2.3 fusion.76
  171.0 2.4 fusion.79
  174.2 3.1 fusion.81
  184.3 28.5 %while.60 = (s32[]{:T(128)}, f32[1024,128]{1,0:T(8,128)S(1)}, f32[1024,128]{1,0:T(8,128)S(1)}, bf16[2,512,1,128]{3,1,0,2:T(8,128)(2,1)}, bf16[2,512,1,128]{3,1,2...) while((s32[]{:T(128)}, f32[1024,128]{1,0:T(8,128)S(1)}, ...), condition=%wide.region_5.5_spmd.clone.clone, body=%wide.region_1.4_spmd.clone.clone.sunk | while | flops 1359025152 | bytes 41875732 | solution.py:104
  186.4 2.3 fusion.76
  191.6 2.4 fusion.79
  194.8 3.1 fusion.81
  200.6 2.3 fusion.76
  205.9 2.4 fusion.79
  209.1 3.1 fusion.81
  216.8 3.4 all-to-all-start.8
  221.8 4.5 %all-to-all-done.8 = bf16[8,2,8192]{2,1,0:T(2,128)(2,1)S(1)} async-done(((bf16[8,2,8192]{2,1,0:T(2,128)(2,1)}), bf16[8,2,8192]{2,1,0:T(2,128)(2,1)S(1)}, u32[]{:S(2)}, u32[]{:S(2)}) %all-to-all-start.8) | async-done | bytes 262176 | tf_op jit(solution)/shard_map/all_to_all | solution.py:172
  226.3 3.6 all-to-all-start.9
  229.9 3.1 copy.153
  233.0 3.2 all-to-all-done.9
  236.2 3.6 all-to-all-start.6
  239.8 1.8 copy.180
  241.6 9.9 %all-to-all-done.6 = bf16[1024,4,128]{2,1,0:T(4,128)(2,1)S(1)} async-done(((bf16[1024,4,128]{2,1,0:T(4,128)(2,1)}), bf16[1024,4,128]{2,1,0:T(4,128)(2,1)S(1)}, u32[]{:S(2)}, u32[]{:S(2)}) %all-to-all-start.6) | async-done | bytes 1048608 | tf_op jit(solution)/shard_map/all_to_all | solution.py:168
  251.5 3.6 all-to-all-start.7
  255.4 1.3 convert_element_type.252
  257.0 1.3 convert_element_type.259
  261.8 1.3 copy.154
  263.1 2.6 reshape.405
  265.7 2.4 all-to-all-done.7
  268.3 1.8 copy.156
  270.1 1.7 bitcast_multiply_fusion
  273.0 3.2 copy.163
  276.2 2.7 pad_maximum_fusion
  278.9 2.0 copy.162
  280.9 3.0 fusion.40
  286.0 90.5 %all-reduce = (f32[4096]{0:T(1024)}, f32[512]{0:T(512)}, f32[512]{0:T(512)}) all-reduce(f32[4096]{0:T(1024)S(1)} %bitcast.274, f32[512]{0:T(512)S(1)} %bitcast.276, f32[512]{0:T(512)S(1)} %bitcast.277), channel_id=1, replica_groups=mesh['dp'=32,'seq'=8] {'dp','seq'}, use_global_device_ids=true, to_apply=%region_10.11 | all-reduce | flops 5120 | bytes 40960 | tf_op jit(solution)/shard_map/psum | solution.py:183
  (290 shorter events, 87.0 us)
Async XLA Ops:
  0.6 10.7 %copy-start.22 = (bf16[1,128,512]{2,1,0:T(8,128)(2,1)S(1)}, bf16[1,128,512]{2,1,0:T(8,128)(2,1)}, u32[]{:S(2)}) copy-start(bf16[1,128,512]{2,1,0:T(8,128)(2,1)} %param.15) | copy-start | bytes 393220
  0.6 10.9 %copy-start.23 = (bf16[1,128,512]{2,1,0:T(8,128)(2,1)S(1)}, bf16[1,128,512]{2,1,0:T(8,128)(2,1)}, u32[]{:S(2)}) copy-start(bf16[1,128,512]{2,1,0:T(8,128)(2,1)} %param.18) | copy-start | bytes 393220
  2.4 16.9 %copy-start.25 = (bf16[512]{0:T(512)(128)(2,1)S(1)}, bf16[512]{0:T(512)(128)(2,1)}, u32[]{:S(2)}) copy-start(bf16[512]{0:T(512)(128)(2,1)} %param.20) | copy-start | bytes 3076
  2.4 12.7 %all-to-all-start.2 = ((bf16[128,8,128]{2,0,1:T(8,128)(2,1)}), bf16[128,8,128]{2,0,1:T(8,128)(2,1)S(1)}, u32[]{:S(2)}, u32[]{:S(2)}) async-start(bf16[128,8,128]{2,0,1:T(8,128)(2,1)} %bitcast.11), calls=%async_computation.2 | async-start | bytes 524288 | tf_op jit(solution)/shard_map/all_to_all | solution.py:158
  12.1 37.5 %copy-start.8 = (f32[128,128]{1,0:T(8,128)}, f32[128,128]{1,0:T(8,128)S(1)}, u32[]{:S(2)}) copy-start(f32[128,128]{1,0:T(8,128)S(1)} %get-tuple-element.735) | copy-start | bytes 196612
  12.1 37.6 %copy-start.6 = (f32[128,128]{1,0:T(8,128)}, f32[128,128]{1,0:T(8,128)S(1)}, u32[]{:S(2)}) copy-start(f32[128,128]{1,0:T(8,128)S(1)} %get-tuple-element.734) | copy-start | bytes 196612
  15.8 9.5 %all-to-all-start.4 = ((bf16[128,8,128]{2,0,1:T(8,128)(2,1)}), bf16[128,8,128]{2,0,1:T(8,128)(2,1)S(1)}, u32[]{:S(2)}, u32[]{:S(2)}) async-start(bf16[128,8,128]{2,0,1:T(8,128)(2,1)} %bitcast.21), calls=%async_computation.4 | async-start | bytes 524288 | tf_op jit(solution)/shard_map/all_to_all | solution.py:159
  19.3 20.5 %copy-start.10 = (bf16[1,128,4096]{2,1,0:T(8,128)(2,1)S(1)}, bf16[1,128,4096]{2,1,0:T(8,128)(2,1)}, u32[]{:S(2)}) copy-start(bf16[1,128,4096]{2,1,0:T(8,128)(2,1)} %param.23) | copy-start | bytes 3145732
  25.3 15.8 %copy-start.13 = (bf16[128,8,128]{2,0,1:T(8,128)(2,1)}, bf16[128,8,128]{2,0,1:T(8,128)(2,1)S(1)}, u32[]{:S(2)}) copy-start(bf16[128,8,128]{2,0,1:T(8,128)(2,1)S(1)} %all-to-all-done.4) | copy-start | bytes 786436
  26.1 9.5 %all-to-all-start.5 = ((bf16[128,8,128]{2,0,1:T(8,128)(2,1)}), bf16[128,8,128]{2,0,1:T(8,128)(2,1)S(1)}, u32[]{:S(2)}, u32[]{:S(2)}) async-start(bf16[128,8,128]{2,0,1:T(8,128)(2,1)} %bitcast.26), calls=%async_computation.5 | async-start | bytes 524288 | tf_op jit(solution)/shard_map/all_to_all | solution.py:154
  35.6 0.8 copy-start.15
  36.4 9.5 %all-to-all-start.3 = ((bf16[128,8,128]{2,0,1:T(8,128)(2,1)}), bf16[128,8,128]{2,0,1:T(8,128)(2,1)S(1)}, u32[]{:S(2)}, u32[]{:S(2)}) async-start(bf16[128,8,128]{2,0,1:T(8,128)(2,1)} %bitcast.17), calls=%async_computation.3 | async-start | bytes 524288 | tf_op jit(solution)/shard_map/all_to_all | solution.py:153
  39.8 10.0 %copy-start.11 = (bf16[1,128,4096]{2,1,0:T(8,128)(2,1)S(1)}, bf16[1,128,4096]{2,1,0:T(8,128)(2,1)}, u32[]{:S(2)}) copy-start(bf16[1,128,4096]{2,1,0:T(8,128)(2,1)} %param.14) | copy-start | bytes 3145732
  45.9 3.8 %copy-start.17 = (bf16[128,8,128]{2,0,1:T(8,128)(2,1)}, bf16[128,8,128]{2,0,1:T(8,128)(2,1)S(1)}, u32[]{:S(2)}) copy-start(bf16[128,8,128]{2,0,1:T(8,128)(2,1)S(1)} %all-to-all-done.3) | copy-start | bytes 786436
  45.9 4.6 %copy-start.24 = (bf16[4096]{0:T(1024)(128)(2,1)S(1)}, bf16[4096]{0:T(1024)(128)(2,1)}, u32[]{:S(2)}) copy-start(bf16[4096]{0:T(1024)(128)(2,1)} %param.19) | copy-start | bytes 24580
  45.9 14.1 %all-to-all-start.1 = ((bf16[128,32,128]{0,2,1:T(8,128)(2,1)}), bf16[128,32,128]{0,2,1:T(8,128)(2,1)S(1)}, u32[]{:S(2)}, u32[]{:S(2)}) async-start(bf16[128,32,128]{0,2,1:T(8,128)(2,1)} %bitcast.6), calls=%async_computation.1 | async-start | bytes 2097152 | tf_op jit(solution)/shard_map/all_to_all | solution.py:155
  49.7 1.7 copy-start.18
  49.8 1.6 copy-start.20
  52.2 11.4 %copy-start.14 = (bf16[128,8,128]{2,0,1:T(8,128)(2,1)S(1)}, bf16[128,8,128]{2,0,1:T(8,128)(2,1)}, u32[]{:S(2)}) copy-start(bf16[128,8,128]{2,0,1:T(8,128)(2,1)} %copy-done.13) | copy-start | bytes 786436
  52.2 11.4 %copy-start.16 = (bf16[128,8,128]{2,0,1:T(8,128)(2,1)S(1)}, bf16[128,8,128]{2,0,1:T(8,128)(2,1)}, u32[]{:S(2)}) copy-start(bf16[128,8,128]{2,0,1:T(8,128)(2,1)} %copy-done.15) | copy-start | bytes 786436
  60.0 13.9 %all-to-all-start = ((bf16[128,32,128]{2,0,1:T(8,128)(2,1)}), bf16[128,32,128]{2,0,1:T(8,128)(2,1)S(1)}, u32[]{:S(2)}, u32[]{:S(2)}) async-start(bf16[128,32,128]{2,0,1:T(8,128)(2,1)} %copy.142), calls=%async_computation | async-start | bytes 2097152 | tf_op jit(solution)/shard_map/all_to_all | solution.py:152
  89.4 3.7 copy-start
  103.7 3.8 copy-start
  108.1 1.0 copy-start.3
  108.1 1.0 copy-start.4
  124.3 3.7 copy-start
  138.6 3.8 copy-start
  143.0 1.0 copy-start.3
  143.0 1.0 copy-start.4
  159.3 3.7 copy-start
  173.5 3.8 copy-start
  177.9 1.0 copy-start.3
  177.9 1.0 copy-start.4
  194.2 3.7 copy-start
  208.4 3.8 copy-start
  212.8 1.0 copy-start.3
  212.8 1.0 copy-start.4
  216.8 9.5 %all-to-all-start.8 = ((bf16[8,2,8192]{2,1,0:T(2,128)(2,1)}), bf16[8,2,8192]{2,1,0:T(2,128)(2,1)S(1)}, u32[]{:S(2)}, u32[]{:S(2)}) async-start(bf16[8,2,8192]{2,1,0:T(2,128)(2,1)} %reshape.436), calls=%async_computation.8 | async-start | bytes 524288 | tf_op jit(solution)/shard_map/all_to_all | solution.py:172
  226.3 10.0 %all-to-all-start.9 = ((bf16[8,2,8192]{2,1,0:T(2,128)(2,1)}), bf16[8,2,8192]{2,1,0:T(2,128)(2,1)S(1)}, u32[]{:S(2)}, u32[]{:S(2)}) async-start(bf16[8,2,8192]{2,1,0:T(2,128)(2,1)} %reshape.438), calls=%async_computation.9 | async-start | bytes 524288 | tf_op jit(solution)/shard_map/all_to_all | solution.py:175
  229.9 9.9 %copy-start.12 = (bf16[4,1024,1,128]{3,1,2,0:T(8,128)(2,1)S(1)}, bf16[4,1024,1,128]{3,1,2,0:T(8,128)(2,1)}, u32[]{:S(2)}) copy-start(bf16[4,1024,1,128]{3,1,2,0:T(8,128)(2,1)} %get-tuple-element.348) | copy-start | bytes 3145732
  236.2 15.3 %all-to-all-start.6 = ((bf16[1024,4,128]{2,1,0:T(4,128)(2,1)}), bf16[1024,4,128]{2,1,0:T(4,128)(2,1)S(1)}, u32[]{:S(2)}, u32[]{:S(2)}) async-start(bf16[1024,4,128]{2,1,0:T(4,128)(2,1)} %copy.153), calls=%async_computation.6 | async-start | bytes 2097152 | tf_op jit(solution)/shard_map/all_to_all | solution.py:168
  251.5 16.6 %all-to-all-start.7 = ((bf16[1024,4,128]{2,1,0:T(4,128)(2,1)}), bf16[1024,4,128]{2,1,0:T(4,128)(2,1)S(1)}, u32[]{:S(2)}, u32[]{:S(2)}) async-start(bf16[1024,4,128]{2,1,0:T(4,128)(2,1)} %bitcast.260), calls=%async_computation.7 | async-start | bytes 2097152 | tf_op jit(solution)/shard_map/all_to_all | solution.py:169
  255.4 5.0 %copy-start.9 = (f32[128,128]{1,0:T(8,128)S(1)}, f32[128,128]{1,0:T(8,128)}, u32[]{:S(2)}) copy-start(f32[128,128]{1,0:T(8,128)} %copy-done.8) | copy-start | bytes 196612
  257.0 3.6 copy-start.7
  258.5 3.1 copy-start.5
  268.3 1.8 copy-start.19
  280.9 3.0 copy-start.1
  280.9 3.5 copy-start.2
  280.9 3.5 copy-start.21
where the time goes:
time: 379 us; the launch traced here: 376 us
  blocking collectives  90.5 us (24%)
  matrix products  79 us (21%)
  local copies, waits for them, and re-layouts  62 us (16%)
  waiting for transfers between devices  53.1 us (14%)
  starting transfers between devices  38.1 us (10%)
  other arithmetic  37.6 us (10%)
  loops' own time  14.1 us (4%)
    psum x1, blocking collectives, body(): lax.psum((jnp.sum(grad_query, axis=0).reshape(HQ * HD), jnp.sum(grad_key,...  90.5 us
    dot_general x8, matrix products, row_step(): jnp.einsum('hrk,kd->rhd', dscore, key_one, preferred_element_type=jnp.flo...  24.6 us
    dot_general x8, matrix products, row_step(): jnp.einsum('rhd,kd->hrk', cot_rows, value_one, preferred_element_type=jnp...  19.4 us
    dot_general x8, matrix products, row_step(): jnp.einsum('rhd,kd->hrk', query_rows, key_one, preferred_element_type=jnp...  18.6 us
    all_to_all x1, waiting for transfers between devices, body(): lax.all_to_all(outputs, 'seq', split_axis=0, concat_axis=1, tiled=True)  9.94 us
    another operation x1, loops' own time, attend(): lax.scan(head_step, (zeros_kv, zeros_kv), jnp.arange(heads // head_block,...  8.13 us
    unnamed x57, local copies, waits for them, and re-layouts  7.6 us
  transfers between devices with their start and end apart: 10, of which 10 were waited for; matrix products, arithmetic and copies ran while one was open for 7% of the time, Pallas kernels for 0%

commit v1 on v0

--- a/solution.py
+++ b/solution.py
@@ -1,3 +1,4 @@
+import functools
 import jax
 import jax.numpy as jnp
 from jax import lax
@@ -7,6 +8,15 @@
 KV = 4
 HD = 128
 GROUP = 8
+
+
+def finish_things_by_axis(xs, row_axis, net_axis):
+    for p in (row_axis, net_axis):
+        xs = lax.psum(xs, p)
+    return xs
+
+
+trees_mix = functools.partial(finish_things_by_axis, row_axis="dp", net_axis="seq")
 
 
 def rotary_tables(positions, width):
@@ -180,13 +190,12 @@
     dv_tokens = jnp.sum(dv_copies.reshape(tokens, KV, copies, HD), axis=2)
     grad_query = rotary_back(dq_tokens.astype(jnp.float32), positions)
     grad_key = rotary_back(dk_tokens, positions)
-    sums_query, sums_key, sums_value = lax.psum(
+    sums_query, sums_key, sums_value = trees_mix(
         (
             jnp.sum(grad_query, axis=0).reshape(HQ * HD),
             jnp.sum(grad_key, axis=0).reshape(KV * HD),
             jnp.sum(dv_tokens, axis=0).reshape(KV * HD),
-        ),
-        ("dp", "seq"),
+        )
     )
     return (
         out_tokens.reshape(1, tokens, HQ * HD),

time: 379 us -> 473 us (1.25)
  the two profiles are of different devices: /device:TPU:1 before, /device:TPU:0 now
where the time goes in v1:
time: 473 us; the launch traced here: 471 us
  blocking collectives  174 us (37%)
  matrix products  78.9 us (17%)
  waiting for transfers between devices  65.3 us (14%)
  local copies, waits for them, and re-layouts  62 us (13%)
  other arithmetic  37.6 us (8%)
  starting transfers between devices  36.2 us (8%)
  loops' own time  14.1 us (3%)
    psum x2, blocking collectives, finish_things_by_axis(): xs = lax.psum(xs, p)  174 us
    dot_general x8, matrix products, row_step(): jnp.einsum('hrk,kd->rhd', dscore, key_one, preferred_element_type=jnp.flo...  24.6 us
    dot_general x8, matrix products, row_step(): jnp.einsum('rhd,kd->hrk', cot_rows, value_one, preferred_element_type=jnp...  19.3 us
    dot_general x8, matrix products, row_step(): jnp.einsum('rhd,kd->hrk', query_rows, key_one, preferred_element_type=jnp...  18.5 us
    all_to_all x1, waiting for transfers between devices, body(): lax.all_to_all(outputs, 'seq', split_axis=0, concat_axis=1, tiled=True)  12.6 us
  transfers between devices with their start and end apart: 10, of which 10 were waited for; matrix products, arithmetic and copies ran while one was open for 6% of the time, Pallas kernels for 0%

profile of v1, /device:TPU:0, one launch (start us, length us, event | category | flops | bytes accessed | tf_op | source)
XLA Modules:
  0.0 470.5 jit_solution(18312971573839053873)
XLA Ops:
  2.4 4.2 all-to-all-start.2
  9.8 4.1 all-to-all-done.2
  14.6 3.4 all-to-all-start.4
  18.1 7.2 %all-to-all-done.4 = bf16[128,8,128]{2,0,1:T(8,128)(2,1)S(1)} async-done(((bf16[128,8,128]{2,0,1:T(8,128)(2,1)}), bf16[128,8,128]{2,0,1:T(8,128)(2,1)S(1)}, u32[]{:S(2)}, u32[]{:S(2)}) %all-to-all-start.4) | async-done | bytes 262176 | tf_op jit(solution)/shard_map/all_to_all | solution.py:169
  26.1 3.4 all-to-all-start.5
  29.8 6.9 %all-to-all-done.5 = bf16[128,8,128]{2,0,1:T(8,128)(2,1)S(1)} async-done(((bf16[128,8,128]{2,0,1:T(8,128)(2,1)}), bf16[128,8,128]{2,0,1:T(8,128)(2,1)S(1)}, u32[]{:S(2)}, u32[]{:S(2)}) %all-to-all-start.5) | async-done | bytes 262176 | tf_op jit(solution)/shard_map/all_to_all | solution.py:164
  37.5 3.4 all-to-all-start.3
  42.3 5.9 %all-to-all-done.3 = bf16[128,8,128]{2,0,1:T(8,128)(2,1)S(1)} async-done(((bf16[128,8,128]{2,0,1:T(8,128)(2,1)}), bf16[128,8,128]{2,0,1:T(8,128)(2,1)S(1)}, u32[]{:S(2)}, u32[]{:S(2)}) %all-to-all-start.3) | async-done | bytes 262176 | tf_op jit(solution)/shard_map/all_to_all | solution.py:163
  48.2 3.7 all-to-all-start.1
  54.5 1.3 copy.142
  55.8 7.9 %all-to-all-done.1 = bf16[128,32,128]{0,2,1:T(8,128)(2,1)S(1)} async-done(((bf16[128,32,128]{0,2,1:T(8,128)(2,1)}), bf16[128,32,128]{0,2,1:T(8,128)(2,1)S(1)}, u32[]{:S(2)}, u32[]{:S(2)}) %all-to-all-start.1) | async-done | bytes 1048608 | tf_op jit(solution)/shard_map/all_to_all | solution.py:165
  63.7 3.6 all-to-all-start
  67.3 1.8 pad_maximum_fusion.1
  70.4 8.3 %all-to-all-done = bf16[128,32,128]{2,0,1:T(8,128)(2,1)S(1)} async-done(((bf16[128,32,128]{2,0,1:T(8,128)(2,1)}), bf16[128,32,128]{2,0,1:T(8,128)(2,1)S(1)}, u32[]{:S(2)}, u32[]{:S(2)}) %all-to-all-start) | async-done | bytes 1048608 | tf_op jit(solution)/shard_map/all_to_all | solution.py:162
  79.9 139.6 %while.59 = (s32[]{:T(128)}, f32[1024,1,128]{2,0,1:T(8,128)S(1)}, f32[1024,1,128]{2,0,1:T(8,128)S(1)}, bf16[4,1024,1,128]{3,1,2,0:T(8,128)(2,1)}, bf16[4,1024,1,...) while((s32[]{:T(128)}, f32[1024,1,128]{2,0,1:T(8,128)S(1)}, ...), condition=%wide.region_6.7_spmd.clone.clone, body=%wide.region_0.6_spmd.clone.clone.sunk | while | flops 1359287296 | bytes 49224388 | solution.py:126
  84.4 28.5 %while.60 = (s32[]{:T(128)}, f32[1024,128]{1,0:T(8,128)S(1)}, f32[1024,128]{1,0:T(8,128)S(1)}, bf16[2,512,1,128]{3,1,0,2:T(8,128)(2,1)}, bf16[2,512,1,128]{3,1,2...) while((s32[]{:T(128)}, f32[1024,128]{1,0:T(8,128)S(1)}, ...), condition=%wide.region_5.5_spmd.clone.clone, body=%wide.region_1.4_spmd.clone.clone.sunk | while | flops 1359025152 | bytes 41875732 | solution.py:114
  86.5 2.3 fusion.76
  91.7 2.4 fusion.79
  95.0 3.1 fusion.81
  100.7 2.3 fusion.76
  106.0 2.4 fusion.79
  109.2 3.1 fusion.81
  119.3 28.5 %while.60 = (s32[]{:T(128)}, f32[1024,128]{1,0:T(8,128)S(1)}, f32[1024,128]{1,0:T(8,128)S(1)}, bf16[2,512,1,128]{3,1,0,2:T(8,128)(2,1)}, bf16[2,512,1,128]{3,1,2...) while((s32[]{:T(128)}, f32[1024,128]{1,0:T(8,128)S(1)}, ...), condition=%wide.region_5.5_spmd.clone.clone, body=%wide.region_1.4_spmd.clone.clone.sunk | while | flops 1359025152 | bytes 41875732 | solution.py:114
  121.4 2.3 fusion.76
  126.6 2.4 fusion.79
  129.9 3.1 fusion.81
  135.6 2.3 fusion.76
  140.9 2.4 fusion.79
  144.1 3.1 fusion.81
  154.2 28.5 %while.60 = (s32[]{:T(128)}, f32[1024,128]{1,0:T(8,128)S(1)}, f32[1024,128]{1,0:T(8,128)S(1)}, bf16[2,512,1,128]{3,1,0,2:T(8,128)(2,1)}, bf16[2,512,1,128]{3,1,2...) while((s32[]{:T(128)}, f32[1024,128]{1,0:T(8,128)S(1)}, ...), condition=%wide.region_5.5_spmd.clone.clone, body=%wide.region_1.4_spmd.clone.clone.sunk | while | flops 1359025152 | bytes 41875732 | solution.py:114
  156.3 2.3 fusion.76
  161.5 2.4 fusion.79
  164.8 3.1 fusion.81
  170.5 2.3 fusion.76
  175.8 2.4 fusion.79
  179.0 3.1 fusion.81
  189.1 28.5 %while.60 = (s32[]{:T(128)}, f32[1024,128]{1,0:T(8,128)S(1)}, f32[1024,128]{1,0:T(8,128)S(1)}, bf16[2,512,1,128]{3,1,0,2:T(8,128)(2,1)}, bf16[2,512,1,128]{3,1,2...) while((s32[]{:T(128)}, f32[1024,128]{1,0:T(8,128)S(1)}, ...), condition=%wide.region_5.5_spmd.clone.clone, body=%wide.region_1.4_spmd.clone.clone.sunk | while | flops 1359025152 | bytes 41875732 | solution.py:114
  191.2 2.3 fusion.76
  196.4 2.4 fusion.79
  199.7 3.1 fusion.81
  205.4 2.3 fusion.76
  210.7 2.4 fusion.79
  213.9 3.1 fusion.81
  221.6 3.4 all-to-all-start.8
  226.6 5.9 %all-to-all-done.8 = bf16[8,2,8192]{2,1,0:T(2,128)(2,1)S(1)} async-done(((bf16[8,2,8192]{2,1,0:T(2,128)(2,1)}), bf16[8,2,8192]{2,1,0:T(2,128)(2,1)S(1)}, u32[]{:S(2)}, u32[]{:S(2)}) %all-to-all-start.8) | async-done | bytes 262176 | tf_op jit(solution)/shard_map/all_to_all | solution.py:182
  232.5 3.6 all-to-all-start.9
  236.1 3.1 copy.153
  239.2 5.6 %all-to-all-done.9 = bf16[8,2,8192]{2,1,0:T(2,128)(2,1)S(1)} async-done(((bf16[8,2,8192]{2,1,0:T(2,128)(2,1)}), bf16[8,2,8192]{2,1,0:T(2,128)(2,1)S(1)}, u32[]{:S(2)}, u32[]{:S(2)}) %all-to-all-start.9) | async-done | bytes 262176 | tf_op jit(solution)/shard_map/all_to_all | solution.py:185
  244.9 3.6 all-to-all-start.6
  248.4 1.8 copy.180
  250.2 12.6 %all-to-all-done.6 = bf16[1024,4,128]{2,1,0:T(4,128)(2,1)S(1)} async-done(((bf16[1024,4,128]{2,1,0:T(4,128)(2,1)}), bf16[1024,4,128]{2,1,0:T(4,128)(2,1)S(1)}, u32[]{:S(2)}, u32[]{:S(2)}) %all-to-all-start.6) | async-done | bytes 1048608 | tf_op jit(solution)/shard_map/all_to_all | solution.py:178
  262.8 3.9 all-to-all-start.7
  267.1 1.3 convert_element_type.252
  268.7 1.3 convert_element_type.259
  273.4 1.3 copy.154
  274.8 2.6 reshape.405
  278.5 1.8 copy.156
  280.3 1.7 bitcast_multiply_fusion
  283.2 3.2 copy.163
  286.4 2.7 pad_maximum_fusion
  289.1 2.0 copy.162
  291.1 3.0 fusion.40
  296.1 139.9 %all-reduce = (f32[4096]{0:T(1024)S(1)}, f32[512]{0:T(512)S(1)}, f32[512]{0:T(512)S(1)}) all-reduce(f32[4096]{0:T(1024)S(1)} %bitcast.274, f32[512]{0:T(512)S(1)} %bitcast.276, f32[512]{0:T(512)S(1)} %bitcast.277), channel_id=1, replica_groups=mesh['dp'=32,'seq'=8] {'dp'}, use_global_device_ids=true, to_apply=%region_10.11 | all-reduce | flops 5120 | bytes 40960 | tf_op jit(solution)/shard_map/psum | solution.py:15
  436.0 34.5 %all-reduce.1 = (f32[4096]{0:T(1024)}, f32[512]{0:T(512)}, f32[512]{0:T(512)}) all-reduce(f32[4096]{0:T(1024)S(1)} %get-tuple-element.709, f32[512]{0:T(512)S(1)} %get-tuple-element.710, f32[512]{0:T(512)S(1)} %get-tuple-element.711), channel_id=1, replica_groups=mesh['dp'=32,'seq'=8] {'seq'}, use_global_device_ids=true, to_apply=%region_11.12 | all-reduce | flops 5120 | bytes 40960 | tf_op jit(solution)/shard_map/psum | solution.py:15
  (291 shorter events, 88.0 us)
Async XLA Ops:
  0.6 8.4 %copy-start.22 = (bf16[1,128,512]{2,1,0:T(8,128)(2,1)S(1)}, bf16[1,128,512]{2,1,0:T(8,128)(2,1)}, u32[]{:S(2)}) copy-start(bf16[1,128,512]{2,1,0:T(8,128)(2,1)} %param.15) | copy-start | bytes 393220
  0.6 8.6 %copy-start.23 = (bf16[1,128,512]{2,1,0:T(8,128)(2,1)S(1)}, bf16[1,128,512]{2,1,0:T(8,128)(2,1)}, u32[]{:S(2)}) copy-start(bf16[1,128,512]{2,1,0:T(8,128)(2,1)} %param.18) | copy-start | bytes 393220
  2.4 15.7 %copy-start.25 = (bf16[512]{0:T(512)(128)(2,1)S(1)}, bf16[512]{0:T(512)(128)(2,1)}, u32[]{:S(2)}) copy-start(bf16[512]{0:T(512)(128)(2,1)} %param.20) | copy-start | bytes 3076
  2.4 11.5 %all-to-all-start.2 = ((bf16[128,8,128]{2,0,1:T(8,128)(2,1)}), bf16[128,8,128]{2,0,1:T(8,128)(2,1)S(1)}, u32[]{:S(2)}, u32[]{:S(2)}) async-start(bf16[128,8,128]{2,0,1:T(8,128)(2,1)} %bitcast.11), calls=%async_computation.2 | async-start | bytes 524288 | tf_op jit(solution)/shard_map/all_to_all | solution.py:168
  9.8 42.0 %copy-start.8 = (f32[128,128]{1,0:T(8,128)}, f32[128,128]{1,0:T(8,128)S(1)}, u32[]{:S(2)}) copy-start(f32[128,128]{1,0:T(8,128)S(1)} %get-tuple-element.738) | copy-start | bytes 196612
  9.8 42.1 %copy-start.6 = (f32[128,128]{1,0:T(8,128)}, f32[128,128]{1,0:T(8,128)S(1)}, u32[]{:S(2)}) copy-start(f32[128,128]{1,0:T(8,128)S(1)} %get-tuple-element.737) | copy-start | bytes 196612
  14.6 10.6 %all-to-all-start.4 = ((bf16[128,8,128]{2,0,1:T(8,128)(2,1)}), bf16[128,8,128]{2,0,1:T(8,128)(2,1)S(1)}, u32[]{:S(2)}, u32[]{:S(2)}) async-start(bf16[128,8,128]{2,0,1:T(8,128)(2,1)} %bitcast.21), calls=%async_computation.4 | async-start | bytes 524288 | tf_op jit(solution)/shard_map/all_to_all | solution.py:169
  18.1 22.8 %copy-start.10 = (bf16[1,128,4096]{2,1,0:T(8,128)(2,1)S(1)}, bf16[1,128,4096]{2,1,0:T(8,128)(2,1)}, u32[]{:S(2)}) copy-start(bf16[1,128,4096]{2,1,0:T(8,128)(2,1)} %param.23) | copy-start | bytes 3145732
  25.3 17.0 %copy-start.13 = (bf16[128,8,128]{2,0,1:T(8,128)(2,1)}, bf16[128,8,128]{2,0,1:T(8,128)(2,1)S(1)}, u32[]{:S(2)}) copy-start(bf16[128,8,128]{2,0,1:T(8,128)(2,1)S(1)} %all-to-all-done.4) | copy-start | bytes 786436
  26.1 10.6 %all-to-all-start.5 = ((bf16[128,8,128]{2,0,1:T(8,128)(2,1)}), bf16[128,8,128]{2,0,1:T(8,128)(2,1)S(1)}, u32[]{:S(2)}, u32[]{:S(2)}) async-start(bf16[128,8,128]{2,0,1:T(8,128)(2,1)} %bitcast.26), calls=%async_computation.5 | async-start | bytes 524288 | tf_op jit(solution)/shard_map/all_to_all | solution.py:164
  36.7 0.8 copy-start.15
  37.5 10.6 %all-to-all-start.3 = ((bf16[128,8,128]{2,0,1:T(8,128)(2,1)}), bf16[128,8,128]{2,0,1:T(8,128)(2,1)S(1)}, u32[]{:S(2)}, u32[]{:S(2)}) async-start(bf16[128,8,128]{2,0,1:T(8,128)(2,1)} %bitcast.17), calls=%async_computation.3 | async-start | bytes 524288 | tf_op jit(solution)/shard_map/all_to_all | solution.py:163
  40.9 11.1 %copy-start.11 = (bf16[1,128,4096]{2,1,0:T(8,128)(2,1)S(1)}, bf16[1,128,4096]{2,1,0:T(8,128)(2,1)}, u32[]{:S(2)}) copy-start(bf16[1,128,4096]{2,1,0:T(8,128)(2,1)} %param.14) | copy-start | bytes 3145732
  48.1 3.8 copy-start.17
  48.1 4.6 copy-start.24
  48.2 15.5 %all-to-all-start.1 = ((bf16[128,32,128]{0,2,1:T(8,128)(2,1)}), bf16[128,32,128]{0,2,1:T(8,128)(2,1)S(1)}, u32[]{:S(2)}, u32[]{:S(2)}) async-start(bf16[128,32,128]{0,2,1:T(8,128)(2,1)} %bitcast.6), calls=%async_computation.1 | async-start | bytes 2097152 | tf_op jit(solution)/shard_map/all_to_all | solution.py:165
  52.0 1.7 copy-start.18
  52.1 1.6 copy-start.20
  54.5 12.8 %copy-start.14 = (bf16[128,8,128]{2,0,1:T(8,128)(2,1)S(1)}, bf16[128,8,128]{2,0,1:T(8,128)(2,1)}, u32[]{:S(2)}) copy-start(bf16[128,8,128]{2,0,1:T(8,128)(2,1)} %copy-done.13) | copy-start | bytes 786436
  54.5 12.8 %copy-start.16 = (bf16[128,8,128]{2,0,1:T(8,128)(2,1)S(1)}, bf16[128,8,128]{2,0,1:T(8,128)(2,1)}, u32[]{:S(2)}) copy-start(bf16[128,8,128]{2,0,1:T(8,128)(2,1)} %copy-done.15) | copy-start | bytes 786436
  63.7 15.0 %all-to-all-start = ((bf16[128,32,128]{2,0,1:T(8,128)(2,1)}), bf16[128,32,128]{2,0,1:T(8,128)(2,1)S(1)}, u32[]{:S(2)}, u32[]{:S(2)}) async-start(bf16[128,32,128]{2,0,1:T(8,128)(2,1)} %copy.142), calls=%async_computation | async-start | bytes 2097152 | tf_op jit(solution)/shard_map/all_to_all | solution.py:162
  94.3 3.7 copy-start
  108.5 3.7 copy-start
  112.9 1.0 copy-start.3
  112.9 1.0 copy-start.4
  129.2 3.7 copy-start
  143.4 3.7 copy-start
  147.8 1.0 copy-start.3
  147.8 1.0 copy-start.4
  164.1 3.7 copy-start
  178.3 3.7 copy-start
  182.7 1.0 copy-start.3
  182.7 1.0 copy-start.4
  199.0 3.7 copy-start
  213.2 3.7 copy-start
  217.6 1.0 copy-start.3
  217.6 1.0 copy-start.4
  221.6 10.9 %all-to-all-start.8 = ((bf16[8,2,8192]{2,1,0:T(2,128)(2,1)}), bf16[8,2,8192]{2,1,0:T(2,128)(2,1)S(1)}, u32[]{:S(2)}, u32[]{:S(2)}) async-start(bf16[8,2,8192]{2,1,0:T(2,128)(2,1)} %reshape.436), calls=%async_computation.8 | async-start | bytes 524288 | tf_op jit(solution)/shard_map/all_to_all | solution.py:182
  232.5 12.4 %all-to-all-start.9 = ((bf16[8,2,8192]{2,1,0:T(2,128)(2,1)}), bf16[8,2,8192]{2,1,0:T(2,128)(2,1)S(1)}, u32[]{:S(2)}, u32[]{:S(2)}) async-start(bf16[8,2,8192]{2,1,0:T(2,128)(2,1)} %reshape.438), calls=%async_computation.9 | async-start | bytes 524288 | tf_op jit(solution)/shard_map/all_to_all | solution.py:185
  236.1 12.3 %copy-start.12 = (bf16[4,1024,1,128]{3,1,2,0:T(8,128)(2,1)S(1)}, bf16[4,1024,1,128]{3,1,2,0:T(8,128)(2,1)}, u32[]{:S(2)}) copy-start(bf16[4,1024,1,128]{3,1,2,0:T(8,128)(2,1)} %get-tuple-element.348) | copy-start | bytes 3145732
  244.9 17.9 %all-to-all-start.6 = ((bf16[1024,4,128]{2,1,0:T(4,128)(2,1)}), bf16[1024,4,128]{2,1,0:T(4,128)(2,1)S(1)}, u32[]{:S(2)}, u32[]{:S(2)}) async-start(bf16[1024,4,128]{2,1,0:T(4,128)(2,1)} %copy.153), calls=%async_computation.6 | async-start | bytes 2097152 | tf_op jit(solution)/shard_map/all_to_all | solution.py:178
  262.8 15.5 %all-to-all-start.7 = ((bf16[1024,4,128]{2,1,0:T(4,128)(2,1)}), bf16[1024,4,128]{2,1,0:T(4,128)(2,1)S(1)}, u32[]{:S(2)}, u32[]{:S(2)}) async-start(bf16[1024,4,128]{2,1,0:T(4,128)(2,1)} %bitcast.260), calls=%async_computation.7 | async-start | bytes 2097152 | tf_op jit(solution)/shard_map/all_to_all | solution.py:179
  267.1 5.0 %copy-start.9 = (f32[128,128]{1,0:T(8,128)S(1)}, f32[128,128]{1,0:T(8,128)}, u32[]{:S(2)}) copy-start(f32[128,128]{1,0:T(8,128)} %copy-done.8) | copy-start | bytes 196612
  268.7 3.6 copy-start.7
  270.2 3.1 copy-start.5
  278.4 1.8 copy-start.19
  291.1 3.0 copy-start.1
  291.1 3.5 copy-start.2
  291.1 3.5 copy-start.21
